TPU v7x, 32 devices: a whole 2x2x4 slice. The times are simulated.
32 devices in a mesh: dp: 16 (over z, y, core), tensor: 2 (over x).
Axes of the slice: x: 2, y: 2, z: 4, core: 2. Of those that a mesh axis runs over, the one named last changes fastest.
Arguments:
- block_input: bfloat16 [160, 197, 768], P('dp'), may hold values from -6 to 6
- image_counts: int32 [16], P('dp'), may hold values from 1 to 10, 88 in all
- first_norm_gain: float32 [768], replicated, may hold values from 0.1 to 1.9
- first_norm_bias: float32 [768], replicated, may hold values from -3 to 3
- w_qkv: bfloat16 [3, 768, 768], P(None, None, 'tensor'), may hold values from -8 to 8
- qv_bias: float32 [2, 768], P(None, 'tensor'), may hold values from -3 to 3
- w_out: bfloat16 [768, 768], P('tensor'), may hold values from -0.75 to 0.75
- b_out: float32 [768], replicated, may hold values from -3 to 3
- second_norm_gain: float32 [768], replicated, may hold values from 0.1 to 1.9
- second_norm_bias: float32 [768], replicated, may hold values from -3 to 3
- w_fc1: bfloat16 [768, 3072], P(None, 'tensor'), may hold values from -0.21875 to 0.21875
- b_fc1: float32 [3072], P('tensor'), may hold values from -3 to 3
- w_fc2: bfloat16 [3072, 768], P('tensor'), may hold values from -0.109375 to 0.109375
- b_fc2: float32 [768], replicated, may hold values from -3 to 3
- cotangent: bfloat16 [160, 197, 768], P('dp'), may hold values from -6 to 6
Outputs:
- block_out: bfloat16 [160, 197, 768], P('dp')
- gradient_of_input: bfloat16 [160, 197, 768], P('dp')
- first_norm_gain_gradient: float32 [768], replicated
- grad_ln1_bias: float32 [768], replicated
- grad_w_qkv: float32 [3, 768, 768], P(None, None, 'tensor')
- grad_qv_bias: float32 [2, 768], P(None, 'tensor')
- grad_w_out: float32 [768, 768], P('tensor')
- grad_b_out: float32 [768], replicated
- second_norm_gain_gradient: float32 [768], replicated
- grad_ln2_bias: float32 [768], replicated
- grad_w_fc1: float32 [768, 3072], P(None, 'tensor')
- grad_b_fc1: float32 [3072], P('tensor')
- grad_w_fc2: float32 [3072, 768], P('tensor')
- grad_b_fc2: float32 [768], replicated
All inputs are finite; a program needn't handle non-finite values. No bound on the sum of `image_counts` on one device may be relied on, other than what follows from the above.
Results may differ from a plain program's by a relative error of at most 0.012.
The roundings to bfloat16 on the way count: a program that leaves them out, or rounds other values in their place, can miss the bound.
Values sent between devices are 32-bit elements; how exact they have to be, the bound alone decides.
No kernel may reach another device: no remote copies, remote signals or barrier semaphores. Data moves between devices by JAX's collectives and lax.ppermute only.
A program may use at most 256 MiB of HBM per device.

v0:
```python
import jax
import jax.numpy as jnp
from jax import lax
from jax.sharding import PartitionSpec as P

HD = 64


EPSILON = 1e-06
INV_ROOT2 = 0.7071067811865476
INV_ROOT2PI = 0.3989422804014327


def apply_layer_norm(values, norm_gain, norm_bias):
    center = jnp.mean(values, -1, keepdims=True)
    shifted = values - center
    spread = jnp.mean(shifted * shifted, -1, keepdims=True)
    inv_std = lax.rsqrt(spread + EPSILON)
    normed = shifted * inv_std
    return (normed * norm_gain + norm_bias, normed, inv_std)


def norm_backward_pass(grad_normed, normed, inv_std, norm_gain):
    scaled = grad_normed * norm_gain
    first = jnp.mean(scaled, -1, keepdims=True)
    second = jnp.mean(scaled * normed, -1, keepdims=True)
    return inv_std * (scaled - first - normed * second)


def gelu_value(pre_act):
    return 0.5 * pre_act * (1.0 + lax.erf(pre_act * INV_ROOT2))


def gelu_slope(pre_act):
    return (
        0.5 * (1.0 + lax.erf(pre_act * INV_ROOT2))
        + pre_act * jnp.exp(-0.5 * pre_act * pre_act) * INV_ROOT2PI
    )


def head_scores(queries, keys_all, scale):
    return (
        jnp.einsum("ishd,ithd->ihst", queries, keys_all, preferred_element_type=jnp.float32) * scale
    )


def shards(
    block_input,
    image_counts,
    first_norm_gain,
    first_norm_bias,
    w_qkv,
    qv_bias,
    w_out,
    b_out,
    second_norm_gain,
    second_norm_bias,
    w_fc1,
    b_fc1,
    w_fc2,
    b_fc2,
    cotangent,
):
    float_thirtytwo = jnp.float32
    bfloat_sixteen = jnp.bfloat16
    image_batch, sequence_length, model_width = block_input.shape
    total_rows = image_batch * sequence_length
    local_heads = w_qkv.shape[2] // HD
    local_width = local_heads * HD
    scale = HD ** (-0.5)
    shape4 = (image_batch, sequence_length, local_heads, HD)
    live_rows = (jnp.arange(total_rows, dtype=jnp.int32) // sequence_length < image_counts[0])[
        :, None
    ]
    input_tokens = block_input.reshape(total_rows, model_width).astype(float_thirtytwo)
    first_normed_tokens, first_centered_scaled, first_inverse_deviation = apply_layer_norm(
        input_tokens, first_norm_gain, first_norm_bias
    )
    normed_one_b = first_normed_tokens.astype(bfloat_sixteen)
    projected = jnp.einsum(
        "nd,cde->cne", normed_one_b, w_qkv, preferred_element_type=float_thirtytwo
    )
    queries = (projected[0] + qv_bias[0]).astype(bfloat_sixteen).reshape(shape4)
    keys_all = projected[1].astype(bfloat_sixteen).reshape(shape4)
    values_all = (projected[2] + qv_bias[1]).astype(bfloat_sixteen).reshape(shape4)
    scores = head_scores(queries, keys_all, scale)
    log_total = jax.nn.logsumexp(scores, axis=-1)
    probs = jnp.exp(scores - log_total[..., None]).astype(bfloat_sixteen)
    context = (
        jnp.einsum("ihst,ithd->ishd", probs, values_all, preferred_element_type=float_thirtytwo)
        .astype(bfloat_sixteen)
        .reshape(total_rows, local_width)
    )
    attn_part = jnp.dot(context, w_out, preferred_element_type=float_thirtytwo)
    attn_full = lax.psum(attn_part, "tensor")
    residual_stream = input_tokens + (attn_full + b_out)
    second_normed_tokens, second_centered_scaled, second_inverse_deviation = apply_layer_norm(
        residual_stream, second_norm_gain, second_norm_bias
    )
    normed_two_b = second_normed_tokens.astype(bfloat_sixteen)
    pre_act = jnp.dot(normed_two_b, w_fc1, preferred_element_type=float_thirtytwo) + b_fc1
    activated = gelu_value(pre_act).astype(bfloat_sixteen)
    mlp_part = jnp.dot(activated, w_fc2, preferred_element_type=float_thirtytwo)
    mlp_full = lax.psum(mlp_part, "tensor")
    outputs = residual_stream + (mlp_full + b_fc2)
    block_out = (
        jnp.where(live_rows, outputs, 0.0)
        .astype(bfloat_sixteen)
        .reshape(image_batch, sequence_length, model_width)
    )
    output_gradient = jnp.where(
        live_rows, cotangent.reshape(total_rows, model_width), jnp.zeros((), bfloat_sixteen)
    )
    grad_w_fc2 = jnp.einsum(
        "nf,nd->fd", activated, output_gradient, preferred_element_type=float_thirtytwo
    )
    grad_b_fc2 = jnp.sum(output_gradient.astype(float_thirtytwo), axis=0)
    grad_act = jnp.einsum(
        "nd,fd->nf", output_gradient, w_fc2, preferred_element_type=float_thirtytwo
    )
    grad_pre = (grad_act * gelu_slope(pre_act)).astype(bfloat_sixteen)
    grad_w_fc1 = jnp.einsum(
        "nd,nf->df", normed_two_b, grad_pre, preferred_element_type=float_thirtytwo
    )
    grad_b_fc1 = jnp.sum(grad_pre.astype(float_thirtytwo), axis=0)
    norm_two_part = jnp.einsum("nf,df->nd", grad_pre, w_fc1, preferred_element_type=float_thirtytwo)
    second_normed_gradient = lax.psum(norm_two_part, "tensor")
    second_norm_gain_gradient = jnp.sum(second_normed_gradient * second_centered_scaled, axis=0)
    grad_ln2_bias = jnp.sum(second_normed_gradient, axis=0)
    residual_gradient = output_gradient.astype(float_thirtytwo) + norm_backward_pass(
        second_normed_gradient, second_centered_scaled, second_inverse_deviation, second_norm_gain
    )
    grad_resid_b = residual_gradient.astype(bfloat_sixteen)
    grad_w_out = jnp.einsum(
        "ne,nd->ed", context, grad_resid_b, preferred_element_type=float_thirtytwo
    )
    grad_b_out = jnp.sum(residual_gradient, axis=0)
    grad_context = (
        jnp.einsum("nd,ed->ne", grad_resid_b, w_out, preferred_element_type=float_thirtytwo)
        .astype(bfloat_sixteen)
        .reshape(shape4)
    )
    probs_full = jnp.exp(head_scores(queries, keys_all, scale) - log_total[..., None])
    probs_again = probs_full.astype(bfloat_sixteen)
    grad_values = jnp.einsum(
        "ihst,ishd->ithd", probs_again, grad_context, preferred_element_type=float_thirtytwo
    ).astype(bfloat_sixteen)
    grad_probs = jnp.einsum(
        "ishd,ithd->ihst", grad_context, values_all, preferred_element_type=float_thirtytwo
    )
    row_dot = jnp.sum(probs_full * grad_probs, axis=-1, keepdims=True)
    grad_scores = (probs_full * (grad_probs - row_dot)).astype(bfloat_sixteen)
    grad_queries = (
        jnp.einsum("ihst,ithd->ishd", grad_scores, keys_all, preferred_element_type=float_thirtytwo)
        * scale
    ).astype(bfloat_sixteen)
    grad_keys = (
        jnp.einsum("ihst,ishd->ithd", grad_scores, queries, preferred_element_type=float_thirtytwo)
        * scale
    ).astype(bfloat_sixteen)
    grad_proj = jnp.stack([grad_queries, grad_keys, grad_values]).reshape(
        3, total_rows, local_width
    )
    grad_w_qkv = jnp.einsum(
        "nd,cne->cde", normed_one_b, grad_proj, preferred_element_type=float_thirtytwo
    )
    grad_qv_bias = jnp.stack(
        [
            jnp.sum(grad_proj[0].astype(float_thirtytwo), axis=0),
            jnp.sum(grad_proj[2].astype(float_thirtytwo), axis=0),
        ]
    )
    norm_one_part = jnp.einsum(
        "cne,cde->nd", grad_proj, w_qkv, preferred_element_type=float_thirtytwo
    )
    first_normed_gradient = lax.psum(norm_one_part, "tensor")
    first_norm_gain_gradient = jnp.sum(first_normed_gradient * first_centered_scaled, axis=0)
    grad_ln1_bias = jnp.sum(first_normed_gradient, axis=0)
    gradient_of_input = (
        (
            residual_gradient
            + norm_backward_pass(
                first_normed_gradient,
                first_centered_scaled,
                first_inverse_deviation,
                first_norm_gain,
            )
        )
        .astype(bfloat_sixteen)
        .reshape(image_batch, sequence_length, model_width)
    )
    summed = lax.psum(
        (
            first_norm_gain_gradient,
            grad_ln1_bias,
            grad_w_qkv,
            grad_qv_bias,
            grad_w_out,
            grad_b_out,
            second_norm_gain_gradient,
            grad_ln2_bias,
            grad_w_fc1,
            grad_b_fc1,
            grad_w_fc2,
            grad_b_fc2,
        ),
        "dp",
    )
    first_norm_gain_gradient, grad_ln1_bias, grad_w_qkv, grad_qv_bias, grad_w_out, grad_b_out = (
        summed[0],
        summed[1],
        summed[2],
        summed[3],
        summed[4],
        summed[5],
    )
    second_norm_gain_gradient, grad_ln2_bias, grad_w_fc1, grad_b_fc1, grad_w_fc2, grad_b_fc2 = (
        summed[6],
        summed[7],
        summed[8],
        summed[9],
        summed[10],
        summed[11],
    )
    return (
        block_out,
        gradient_of_input,
        first_norm_gain_gradient,
        grad_ln1_bias,
        grad_w_qkv,
        grad_qv_bias,
        grad_w_out,
        grad_b_out,
        second_norm_gain_gradient,
        grad_ln2_bias,
        grad_w_fc1,
        grad_b_fc1,
        grad_w_fc2,
        grad_b_fc2,
    )


def solution(mesh):
    in_specs = (
        P("dp", None, None),
        P("dp"),
        P(),
        P(),
        P(None, None, "tensor"),
        P(None, "tensor"),
        P("tensor", None),
        P(),
        P(),
        P(),
        P(None, "tensor"),
        P("tensor"),
        P("tensor", None),
        P(),
        P("dp", None, None),
    )
    out_specs = (
        P("dp", None, None),
        P("dp", None, None),
        P(),
        P(),
        P(None, None, "tensor"),
        P(None, "tensor"),
        P("tensor", None),
        P(),
        P(),
        P(),
        P(None, "tensor"),
        P("tensor"),
        P("tensor", None),
        P(),
    )
    return jax.shard_map(shards, mesh=mesh, in_specs=in_specs, out_specs=out_specs, check_vma=False)
```

profile of v0, /device:TPU:0, one launch (start us, length us, event | category | flops | bytes accessed | tf_op | source)
XLA Modules:
  0.0 1189.8 jit_solution(15098997224716500326)
XLA Ops:
  7.3 6.9 reshape.188
  19.7 7.4 convolution_bitcast_fusion
  35.0 8.1 squeeze.14
  68.6 8.1 squeeze.13
  79.9 8.9 convert_bitcast_fusion.1
  91.8 6.0 reshape.183
  108.3 146.6 %all-reduce.8.cloned.1.call-done = f32[1970,768]{1,0:T(8,128)} async-done(((f32[1970,768]{1,0:T(8,128)}), f32[1970,768]{1,0:T(8,128)}) %all-reduce.8.cloned.1.call-update) | async-done | bytes 6051856 | tf_op jit(solution)/shard_map/psum | solution.py:95
  261.1 8.0 multiply_convert_fusion.1
  269.1 9.3 convert_reduce_fusion
  281.0 6.8 fusion.39
  287.8 10.4 fusion.29
  298.2 8.9 fusion.32
  307.1 129.8 %all-reduce.10.cloned.1.call-done = f32[1970,768]{1,0:T(8,128)} async-done(((f32[1970,768]{1,0:T(8,128)}), f32[1970,768]{1,0:T(8,128)}) %all-reduce.10.cloned.1.call-update) | async-done | bytes 6051856 | tf_op jit(solution)/shard_map/psum | solution.py:127
  436.9 6.0 multiply_reduce_fusion.3
  444.1 5.8 fusion.34
  463.5 8.5 convert_reduce_fusion.2
  472.0 12.1 %multiply_reduce_fusion = (f32[10,6,197]{2,1,0:T(8,128)S(1)}, f32[10,6,197,197]{2,3,1,0:T(8,128)}) fusion(f32[10,6,197,197]{2,3,1,0:T(8,128)} %copy-done.2, f32[10,6,197]{2,1,0:T(8,128)S(1)} %log_add_fusion, bf16[10,197,6,64]{1,3,2,0:T(8,128)(2,1)S(1)} %copy.49, bf16[10,197,6,64]{1,0,3,2:T(8,128)(2,1)} %copy-done.11), kind=kOutput, calls=%fused_computation.2 | convolution fusion | flops 307355456 | bytes 21748800 | tf_op jit(solution)/shard_map/ishd,ithd->ihst/dot_general | solution.py:148
  484.1 6.5 multiply_convert_fusion
  498.4 5.8 copy.70
  504.2 6.0 reshape.193
  510.1 5.9 copy.69
  516.1 6.0 reshape.192
  526.4 6.1 reshape.191
  538.2 9.1 convolution_bitcast_fusion.2
  547.4 11.2 fusion.38
  558.6 6.2 convolution_bitcast_fusion.1
  567.3 236.8 %all-reduce.12.cloned.1.call-done = (f32[3,768,384]{1,2,0:T(8,128)}, f32[384,768]{1,0:T(8,128)}, f32[768,1536]{1,0:T(8,128)}, f32[1536,768]{1,0:T(8,128)}) async-done(((f32[3,768,384]{1,2,0:T(8,128)}, f32[384,768]{1,0:T(8,128)}, f32[768,1536]{1,0:T(8,128)}, f32[1536,768]{1,0:T(8,128)}), (f32[3,768,384]{1,2,0:T(8,128)}, f32[384,768]{1,0:T(8,128)}, f32[768,1536]{1,0:T(8,128)}, ...) | async-done | bytes 14155792 | tf_op jit(solution)/shard_map/psum | solution.py:192
  809.3 275.8 %all-reduce.14.cloned.1.call-done = (f32[1970,768]{1,0:T(8,128)}, f32[1970,768]{1,0:T(8,128)}) async-done(((f32[1970,768]{1,0:T(8,128)}, f32[1970,768]{1,0:T(8,128)}), (f32[1970,768]{1,0:T(8,128)}, f32[1970,768]{1,0:T(8,128)})) %all-reduce.14.cloned.1.call-update) | async-done | bytes 12103696 | tf_op jit(solution)/shard_map/psum | solution.py:104
  1085.2 5.9 multiply_reduce_fusion.4
  1091.4 6.7 add_convert_fusion.2
  1102.1 6.6 select_convert_fusion
  1112.8 61.7 %all-reduce = (f32[768]{0:T(1024)}, f32[768]{0:T(1024)}, f32[2,384]{1,0:T(2,128)}, f32[768]{0:T(1024)}, f32[768]{0:T(1024)}, /*index=5*/f32[768]{0:T(1024)}, f32[1536]{0:T(1024)}, f32[768]{0:T(1024)}) all-reduce(f32[768]{0:T(1024)S(1)} %get-tuple-element.44, ...), channel_id=1, replica_groups=mesh['dp'=16,'tensor'=2] {'dp'}, use_global_device_ids=true, to_apply=%region_16.17 | all-reduce | flops 6912 | bytes 55296 | tf_op jit(solution)/shard_map/psum | solution.py:192
  (149 shorter events, 120.5 us)
Async XLA Ops:
  7.2 253.9 %copy-start = (bf16[768,1536]{1,0:T(8,128)(2,1)S(1)}, bf16[768,1536]{1,0:T(8,128)(2,1)}, u32[]{:S(2)}) copy-start(bf16[768,1536]{1,0:T(8,128)(2,1)} %param.25) | copy-start | bytes 7077892
  7.2 12.5 %copy-start.24 = (f32[768]{0:T(1024)S(1)}, f32[768]{0:T(1024)}, u32[]{:S(2)}) copy-start(f32[768]{0:T(1024)} %param.17) | copy-start | bytes 9220
  7.2 12.5 %copy-start.34 = (f32[768]{0:T(1024)S(1)}, f32[768]{0:T(1024)}, u32[]{:S(2)}) copy-start(f32[768]{0:T(1024)} %param.18) | copy-start | bytes 9220
  7.2 247.7 %all-reduce.8.cloned.1.call-start = ((), (), s32[]{:S(2)}) async-start(), calls=%async_computation | async-start | bytes 12140544 | tf_op jit(solution)/shard_map/psum | solution.py:95
  19.5 7.6 copy-start.20
  19.7 7.5 copy-start.22
  35.0 8.1 copy-start.29
  79.9 8.9 copy-start.11
  88.8 9.0 copy-start.16
  103.5 151.4 %copy-start.27 = (f32[768]{0:T(1024)S(1)}, f32[768]{0:T(1024)}, u32[]{:S(2)}) copy-start(f32[768]{0:T(1024)} %param.22) | copy-start | bytes 9220
  103.5 333.4 %all-reduce.10.cloned.1.call-start = ((), (), s32[]{:S(2)}) async-start(), calls=%async_computation.1 | async-start | bytes 12140544 | tf_op jit(solution)/shard_map/psum | solution.py:127
  260.1 9.0 copy-start.3
  261.1 8.1 copy-start.13
  261.1 8.1 copy-start.30
  287.8 516.4 %all-reduce.12.cloned.1.call-start = ((), (), s32[]{:S(2)}) async-start(), calls=%async_computation.2 | async-start | bytes 28311552 | tf_op jit(solution)/shard_map/psum | solution.py:192
  287.8 10.4 copy-start.37
  436.9 7.1 copy-start.14
  463.5 20.6 %slice-start = ((s8[12288000]{0:T(1024)(128)(4,1)}), s8[4194304]{0:T(1024)(128)(4,1)S(1)}, s32[]{:S(2)}) async-start(s8[12288000]{0:T(1024)(128)(4,1)} %bitcast.49), calls=%async_computation.4 | async-start | bytes 8388608
  463.5 20.6 %slice-start.1 = ((s8[12288000]{0:T(1024)(128)(4,1)}), s8[4194304]{0:T(1024)(128)(4,1)S(1)}, s32[]{:S(2)}) async-start(s8[12288000]{0:T(1024)(128)(4,1)} %bitcast.49), calls=%async_computation.5 | async-start | bytes 8388608
  472.0 12.1 %slice-start.2 = ((s8[12288000]{0:T(1024)(128)(4,1)}), s8[3899392]{0:T(1024)(128)(4,1)S(1)}, s32[]{:S(2)}) async-start(s8[12288000]{0:T(1024)(128)(4,1)} %bitcast.49), calls=%async_computation.6 | async-start | bytes 7798784
  510.1 11.9 %copy-start.12 = (bf16[10,197,6,64]{1,3,2,0:T(8,128)(2,1)S(1)}, bf16[10,197,6,64]{1,3,2,0:T(8,128)(2,1)}, u32[]{:S(2)}) copy-start(bf16[10,197,6,64]{1,3,2,0:T(8,128)(2,1)} %get-tuple-element.81) | copy-start | bytes 4538884
  526.4 9.3 copy-start.15
  526.4 11.8 copy-start.21
  526.4 11.8 copy-start.23
  526.4 11.8 copy-start.25
  526.4 11.8 copy-start.35
  547.3 537.8 %all-reduce.14.cloned.1.call-start = ((), (), s32[]{:S(2)}) async-start(), calls=%async_computation.3 | async-start | bytes 24281088 | tf_op jit(solution)/shard_map/psum | solution.py:104
  547.4 11.2 copy-start.19
  547.4 11.2 copy-start.31
  1108.7 65.9 %copy-start.17 = (f32[384,768]{1,0:T(8,128)S(1)}, f32[384,768]{1,0:T(8,128)}, u32[]{:S(2)}) copy-start(f32[384,768]{1,0:T(8,128)} %get-tuple-element.92) | copy-start | bytes 3538948
  1112.8 67.8 %slice-start.3 = ((s8[4718592]{0:T(1024)(128)(4,1)}), s8[524288]{0:T(1024)(128)(4,1)S(1)}, s32[]{:S(2)}) async-start(s8[4718592]{0:T(1024)(128)(4,1)} %bitcast.51), calls=%async_computation.7 | async-start | bytes 1048576
  1175.6 7.2 copy-start.1
  (15 other events, 53.3 us)
Sparse Core Ops, SparseCore 0:
  103.6 151.1 all-reduce.7
  287.9 149.0 all-reduce.9
  547.5 256.6 all-reduce.11
  806.5 278.5 all-reduce.13
where the time goes:
time: 1200 us; the launch traced here: 1190 us
  waiting for transfers between devices  789 us (66%)
  local copies, waits for them, and re-layouts  135 us (11%)
  matrix products  128 us (11%)
  blocking collectives  61.7 us (5%)
  other arithmetic  60.7 us (5%)
  between operations  15.4 us (1%)
    psum x1, waiting for transfers between devices, shards(): mlp_full = lax.psum(mlp_part, 'tensor')  276 us
    psum x1, waiting for transfers between devices, shards(): lax.psum((first_norm_gain_gradient, grad_ln1_bias, grad_w_qkv, grad_qv_bi...  237 us
    psum x1, waiting for transfers between devices, shards(): attn_full = lax.psum(attn_part, 'tensor')  147 us
    psum x1, waiting for transfers between devices, shards(): second_normed_gradient = lax.psum(norm_two_part, 'tensor')  130 us
    psum x1, blocking collectives, shards(): lax.psum((first_norm_gain_gradient, grad_ln1_bias, grad_w_qkv, grad_qv_bi...  61.7 us
    another operation x7, local copies, waits for them, and re-layouts, shards(): jnp.stack([grad_queries, grad_keys, grad_values])  34.4 us
    unnamed x92, local copies, waits for them, and re-layouts  24.3 us
  transfers between devices with their start and end apart: 4, of which 4 were waited for; matrix products, arithmetic and copies ran while one was open for 4% of the time, Pallas kernels for 0%

commit v1 on v0

v1 whole, which is shorter than its diff:
```python
import functools

import jax
import jax.numpy as jnp
from jax import lax
from jax.experimental import pallas as pl
from jax.experimental.pallas import tpu as pltpu
from jax.sharding import PartitionSpec as P

HD = 64
EPSILON = 1e-06
INV_ROOT2 = 0.7071067811865476
INV_ROOT2PI = 0.3989422804014327
F32 = jnp.float32
BF16 = jnp.bfloat16
IB = 2
LANES = 128
TILE = 256
VMEM_LIMIT = 60 * 1024 * 1024


def _nn(a, b):
    return lax.dot_general(a, b, (((1,), (0,)), ((), ())), preferred_element_type=F32)


def _nt(a, b):
    return lax.dot_general(a, b, (((1,), (1,)), ((), ())), preferred_element_type=F32)


def _tn(a, b):
    return lax.dot_general(a, b, (((0,), (0,)), ((), ())), preferred_element_type=F32)


def norm_stats(values):
    center = jnp.mean(values, -1, keepdims=True)
    shifted = values - center
    spread = jnp.mean(shifted * shifted, -1, keepdims=True)
    inv_std = lax.rsqrt(spread + EPSILON)
    return shifted * inv_std, inv_std


def norm_backward(grad_normed, normed, inv_std, gain):
    scaled = grad_normed * gain
    first = jnp.mean(scaled, -1, keepdims=True)
    second = jnp.mean(scaled * normed, -1, keepdims=True)
    return inv_std * (scaled - first - normed * second)


def row_sum(values):
    return jnp.sum(values, axis=0, keepdims=True)


def stack_heads(two):
    lane = lax.broadcasted_iota(jnp.int32, two.shape, 1)
    zero = jnp.zeros_like(two)
    return jnp.concatenate([jnp.where(lane < HD, two, zero), jnp.where(lane < HD, zero, two)], 0)


def merge_heads(stacked):
    rows = stacked.shape[0] // 2
    lane = lax.broadcasted_iota(jnp.int32, (rows, LANES), 1)
    return jnp.where(lane < HD, stacked[:rows], stacked[rows:])


def pair_probs(queries, keys, seq):
    scores = _nt(queries, keys) * (HD**-0.5)
    column = lax.broadcasted_iota(jnp.int32, scores.shape, 1)
    scores = jnp.where(column < seq, scores, jnp.finfo(F32).min)
    top = jnp.max(scores, -1, keepdims=True)
    weights = jnp.exp(scores - top)
    return weights * (1.0 / jnp.sum(weights, -1, keepdims=True))


def attention(qkv_ref, ctx_ref, seq):
    width = ctx_ref.shape[-1]
    for i in range(IB):
        for pair in range(width // LANES):
            at = [pl.ds(part * width + pair * LANES, LANES) for part in range(3)]
            probs = pair_probs(stack_heads(qkv_ref[i, :, at[0]]), qkv_ref[i, :, at[1]], seq)
            context = _nn(probs.astype(BF16), qkv_ref[i, :, at[2]])
            ctx_ref[i, :, pl.ds(pair * LANES, LANES)] = merge_heads(context).astype(BF16)


def project(normed, wcat_ref, qv_ref, qkv_ref):
    width = wcat_ref.shape[1] // 3
    rows = qkv_ref.shape[1]
    out = _nn(normed, wcat_ref[...])
    for part in range(3):
        piece = out[:, part * width : (part + 1) * width]
        if part != 1:
            piece = piece + qv_ref[part // 2 : part // 2 + 1, :]
        qkv_ref[:, :, pl.ds(part * width, width)] = piece.astype(BF16).reshape(IB, rows, width)


def load_images(x_ref, xs_ref):
    seq, rows = x_ref.shape[1], xs_ref.shape[0] // IB
    for i in range(IB):
        xs_ref[i * rows : i * rows + seq, :] = x_ref[i]
    return xs_ref[...].astype(F32)


def first_kernel(
    scal, x, cot, g1, b1, w_qkv, qv, w_out, n1_o, qkv_o, ctx_o, part_o, g_o, xs, wcat
):
    step = pl.program_id(0)
    width = w_out.shape[0]
    rows, model = n1_o.shape[1:]
    seq = x.shape[1]

    @pl.when(step == 0)
    def _():
        xs[...] = jnp.zeros_like(xs)
        for part in range(3):
            wcat[:, part * width : (part + 1) * width] = w_qkv[part]

    xhat, _ = norm_stats(load_images(x, xs))
    normed = (xhat * g1[...] + b1[...]).astype(BF16)
    n1_o[...] = normed.reshape(IB, rows, model)
    project(normed, wcat, qv, qkv_o)
    attention(qkv_o, ctx_o, seq)
    part_o[...] = _nn(ctx_o[...].reshape(IB * rows, width), w_out[...]).reshape(part_o.shape)
    g_o[...] = jnp.zeros_like(g_o)
    for i in range(IB):
        live = step * IB + i < scal[0]
        g_o[i, 0:seq, :] = jnp.where(live, cot[i], jnp.zeros_like(cot[i]))


def second_kernel(pieces, scal, n1, x, part, qv, b_out, g2, b2, *refs):
    wq_p, wo_p = refs[:pieces], refs[pieces : 2 * pieces]
    qkv_o, ctx_o, wcat, wout, resid_o, n2_o, xs = refs[2 * pieces :]
    step = pl.program_id(0)
    width = wout.shape[0]
    rows, model = n1.shape[1:]
    seq = x.shape[1]

    @pl.when(step == 0)
    def _():
        xs[...] = jnp.zeros_like(xs)
        for p in range(pieces):
            at = p ^ scal[1]
            high = wq_p[p].shape[1]
            where = pl.ds(pl.multiple_of(at * high, 16), high)
            for part in range(3):
                wcat[where, part * width : (part + 1) * width] = wq_p[p][part].astype(BF16)
            high = wo_p[p].shape[0]
            wout[pl.ds(pl.multiple_of(at * high, 16), high), :] = wo_p[p][...].astype(BF16)

    project(n1[...].reshape(IB * rows, model), wcat, qv, qkv_o)
    attention(qkv_o, ctx_o, seq)
    full = part[...].reshape(IB * rows, model) + _nn(
        ctx_o[...].reshape(IB * rows, width), wout[...]
    )
    resid = load_images(x, xs) + (full + b_out[...])
    resid_o[...] = resid.reshape(resid_o.shape)
    xhat, _ = norm_stats(resid)
    n2_o[...] = (xhat * g2[...] + b2[...]).astype(BF16).reshape(n2_o.shape)


def gelu_and_slope(pre):
    bell = 0.5 * (1.0 + lax.erf(pre * INV_ROOT2))
    return pre * bell, bell + pre * jnp.exp(-0.5 * pre * pre) * INV_ROOT2PI


def split_blocks(me, full, send, keep):
    half, high = keep.shape[:2]
    for p in range(half):
        for ref, at in ((keep, p), (send, p + half)):
            ref[p] = full[pl.ds(pl.multiple_of((at ^ me) * high, 8), high), :]


def mlp_a_kernel(scal, n2, fc1, bfc1, g_all, act_o, slope_o, send, keep, act_all, full):
    step = pl.program_id(0)
    rows, model = n2.shape[1:]
    tokens = n2[...].reshape(IB * rows, model)
    here = pl.ds(pl.multiple_of(step * IB * rows, 16), IB * rows)
    for j in range(fc1.shape[1] // TILE):
        cols = pl.ds(j * TILE, TILE)
        act, slope = gelu_and_slope(_nn(tokens, fc1[:, cols]) + bfc1[:, cols])
        act = act.astype(BF16)
        act_all[here, cols] = act
        act_o[:, :, cols] = act.reshape(IB, rows, TILE)
        slope_o[:, :, cols] = slope.reshape(IB, rows, TILE)

    @pl.when(step == pl.num_programs(0) - 1)
    def _():
        strip = 384
        for r in range(full.shape[0] // strip):
            cols = pl.ds(r * strip, strip)
            full[cols, :] = _tn(act_all[:, cols], g_all[...])
        split_blocks(scal[2], full, send, keep)


def mlp_b_kernel(
    scal, act, slope, g, n2_all, fc1, fc2, mlp_o, gn2_o, send, keep, gb_o, gpre_all, full
):
    step = pl.program_id(0)
    rows, model = g.shape[1:]
    hidden = fc1.shape[1]
    here = pl.ds(pl.multiple_of(step * IB * rows, 16), IB * rows)

    @pl.when(step == 0)
    def _():
        gb_o[...] = jnp.zeros_like(gb_o)

    grad_out = g[...].reshape(IB * rows, model)
    for j in range(hidden // TILE):
        cols = pl.ds(j * TILE, TILE)
        grad = _nt(grad_out, fc2[cols, :]) * slope[:, :, cols].reshape(IB * rows, TILE)
        grad = grad.astype(BF16)
        gpre_all[here, cols] = grad
        gb_o[:, cols] += row_sum(grad.astype(F32))
    mlp_o[...] = _nn(act[...].reshape(IB * rows, hidden), fc2[...]).reshape(mlp_o.shape)
    gn2_o[...] = _nt(gpre_all[here, :], fc1[...]).reshape(gn2_o.shape)

    @pl.when(step == pl.num_programs(0) - 1)
    def _():
        strip = 384
        for r in range(full.shape[0] // strip):
            cols = pl.ds(r * strip, strip)
            full[cols, :] = _tn(n2_all[:, cols], gpre_all[...])
        split_blocks(scal[3], full, send, keep)


def mlp_c_kernel(pieces, scal, n2, g, resid, mlp_p, gn2_p, bfc1, g2, bfc2, *refs):
    fc1_p, fc2_p = refs[:pieces], refs[pieces : 2 * pieces]
    out_o, gr_o, grb_o, sums, fc1, fc2, gpre, act_s = refs[2 * pieces :]
    step = pl.program_id(0)
    rows, model = n2.shape[1:]
    hidden = fc1.shape[1]
    seq = out_o.shape[1]

    @pl.when(step == 0)
    def _():
        sums[...] = jnp.zeros_like(sums)
        for p in range(pieces):
            at = p ^ scal[4]
            for source, target in ((fc1_p[p], fc1), (fc2_p[p], fc2)):
                high = source.shape[0]
                target[pl.ds(pl.multiple_of(at * high, 16), high), :] = source[...].astype(BF16)

    tokens = n2[...].reshape(IB * rows, model)
    grad_out = g[...].reshape(IB * rows, model)
    for j in range(hidden // TILE):
        cols = pl.ds(j * TILE, TILE)
        act, slope = gelu_and_slope(_nn(tokens, fc1[:, cols]) + bfc1[:, cols])
        act_s[:, cols] = act.astype(BF16)
        gpre[:, cols] = (_nt(grad_out, fc2[cols, :]) * slope).astype(BF16)
    mlp_full = mlp_p[...].reshape(IB * rows, model) + _nn(act_s[...], fc2[...])
    gn2 = gn2_p[...].reshape(IB * rows, model) + _nt(gpre[...], fc1[...])
    residual = resid[...].reshape(IB * rows, model)
    out = residual + (mlp_full + bfc2[...])
    for i in range(IB):
        live = step * IB + i < scal[0]
        out_o[i] = jnp.where(live, out[i * rows : i * rows + seq], 0.0).astype(BF16)
    xhat, inv = norm_stats(residual)
    grad_f = grad_out.astype(F32)
    grad_resid = grad_f + norm_backward(gn2, xhat, inv, g2[...])
    sums[0:1] += row_sum(gn2 * xhat)
    sums[1:2] += row_sum(gn2)
    sums[2:3] += row_sum(grad_resid)
    sums[3:4] += row_sum(grad_f)
    gr_o[...] = grad_resid.reshape(gr_o.shape)
    grb_o[...] = grad_resid.astype(BF16).reshape(grb_o.shape)


def attention_backward(qkv_ref, gctx, dq_ref, start, seq):
    width = gctx.shape[1]
    rows = qkv_ref.shape[1]
    scale = HD**-0.5
    for i in range(IB):
        where = pl.ds(pl.multiple_of(start + i * rows, 16), rows)
        for pair in range(width // LANES):
            at = [pl.ds(part * width + pair * LANES, LANES) for part in range(3)]
            queries = stack_heads(qkv_ref[i, :, at[0]])
            keys, values = qkv_ref[i, :, at[1]], qkv_ref[i, :, at[2]]
            probs = pair_probs(queries, keys, seq)
            grad = stack_heads(
                gctx[i * rows : (i + 1) * rows, pair * LANES : (pair + 1) * LANES]
            )
            grad_probs = _nt(grad, values)
            dot = jnp.sum(probs * grad_probs, -1, keepdims=True)
            grad_scores = (probs * (grad_probs - dot)).astype(BF16)
            dq_ref[where, at[2]] = _tn(probs.astype(BF16), grad).astype(BF16)
            dq_ref[where, at[0]] = merge_heads(_nn(grad_scores, keys) * scale).astype(BF16)
            dq_ref[where, at[1]] = (_tn(grad_scores, queries) * scale).astype(BF16)


def own_backward_kernel(
    seq,
    scal,
    grb,
    qkv,
    w_qkv,
    w_out,
    n1_all,
    ctx_all,
    grb_all,
    gn1_o,
    send,
    keep,
    gqv_o,
    dq_all,
    wcat,
    full_q,
    full_o,
):
    step = pl.program_id(0)
    rows, model = grb.shape[1:]
    width = w_out.shape[0]

    @pl.when(step == 0)
    def _():
        gqv_o[...] = jnp.zeros_like(gqv_o)
        for part in range(3):
            wcat[:, part * width : (part + 1) * width] = w_qkv[part]

    start = step * IB * rows
    here = pl.ds(pl.multiple_of(start, 16), IB * rows)
    gctx = _nt(grb[...].reshape(IB * rows, model), w_out[...]).astype(BF16)
    attention_backward(qkv, gctx, dq_all, start, seq)
    gn1_o[...] = _nt(dq_all[here, :], wcat[...]).reshape(gn1_o.shape)
    gqv_o[0:1] += row_sum(dq_all[here, 0:width].astype(F32))
    gqv_o[1:2] += row_sum(dq_all[here, 2 * width : 3 * width].astype(F32))

    @pl.when(step == pl.num_programs(0) - 1)
    def _():
        for part in range(3):
            cols = pl.ds(part * width, width)
            full_q[pl.ds(part * model, model), :] = _tn(n1_all[...], dq_all[:, cols])
        full_o[...] = _tn(ctx_all[...], grb_all[...])
        half = keep.shape[0]
        high_q, high_o = full_q.shape[0] // (2 * half), width // (2 * half)
        for p in range(half):
            for ref, at in ((keep, p), (send, p + half)):
                block = at ^ scal[5]
                from_q = pl.ds(pl.multiple_of(block * high_q, 8), high_q)
                from_o = pl.ds(pl.multiple_of(block * high_o, 8), high_o)
                ref[p, 0:high_q, :] = full_q[from_q, :]
                for c in range(model // width):
                    ref[p, high_q + c * high_o : high_q + (c + 1) * high_o, :] = full_o[
                        from_o, c * width : (c + 1) * width
                    ]


def other_backward_kernel(
    scal, grb, qkv, wcat, w_out, gn1_p, gr, x, g1, gin_o, sums, dq, xs
):
    step = pl.program_id(0)
    rows, model = grb.shape[1:]
    seq = x.shape[1]

    @pl.when(step == 0)
    def _():
        sums[...] = jnp.zeros_like(sums)
        xs[...] = jnp.zeros_like(xs)

    gctx = _nt(grb[...].reshape(IB * rows, model), w_out[...]).astype(BF16)
    attention_backward(qkv, gctx, dq, 0, seq)
    gn1 = gn1_p[...].reshape(IB * rows, model) + _nt(dq[...], wcat[...])
    xhat, inv = norm_stats(load_images(x, xs))
    sums[0:1] += row_sum(gn1 * xhat)
    sums[1:2] += row_sum(gn1)
    grad = gr[...].reshape(IB * rows, model) + norm_backward(gn1, xhat, inv, g1[...])
    for i in range(IB):
        gin_o[i] = grad[i * rows : i * rows + seq].astype(BF16)


def portion_kernel(count, scal, *refs):
    for source, target in zip(refs[:count], refs[count:]):
        axis = len(source.shape) - 2
        high = target.shape[axis]
        where = pl.ds(pl.multiple_of(scal[0] * high, 16), high)
        if axis:
            target[...] = source[:, where, :].astype(F32)
        else:
            target[...] = source[where, :].astype(F32)


def _whole(shape):
    return pl.BlockSpec(shape, lambda i, *_: (0,) * len(shape), pipeline_mode=pl.Buffered(1))


def _images(*tail):
    return pl.BlockSpec((IB,) + tail, lambda i, *_: (i,) + (0,) * len(tail))


def _acc(shape):
    return pl.BlockSpec(shape, lambda i, *_: (0,) * len(shape))


def _call(kernel, name, grid, scalars, ins, outs, scratch, flops):
    moved = sum(a.size * a.dtype.itemsize for a, _ in ins)
    return pl.pallas_call(
        kernel,
        name=name,
        grid_spec=pltpu.PrefetchScalarGridSpec(
            num_scalar_prefetch=1,
            grid=(grid,),
            in_specs=[spec for _, spec in ins],
            out_specs=[spec for _, _, spec in outs],
            scratch_shapes=scratch,
        ),
        out_shape=[jax.ShapeDtypeStruct(shape, dtype) for shape, dtype, _ in outs],
        compiler_params=pltpu.CompilerParams(
            dimension_semantics=("arbitrary",), vmem_limit_bytes=VMEM_LIMIT
        ),
        cost_estimate=pl.CostEstimate(
            flops=int(flops), bytes_accessed=int(2 * moved), transcendentals=0
        ),
    )(scalars, *[a for a, _ in ins])


class Exchange:
    def __init__(self, size):
        self.size = size
        self.bits = size.bit_length() - 1

    def swap(self, value, bit):
        pairs = [(i, i ^ (1 << bit)) for i in range(self.size)]
        return lax.ppermute(value, "dp", pairs)

    def relative(self, index, order):
        out = jnp.int32(0)
        for bit in order:
            out = out * 2 + ((index >> bit) & 1)
        return out

    def reduce(self, send, keep, order):
        for n, bit in enumerate(order):
            got = self.swap(send, bit)
            half = keep.shape[0] // 2
            if n + 1 < len(order):
                send, keep = keep[half:] + got[half:], keep[:half] + got[:half]
            else:
                keep = keep + got
        for bit in range(self.bits):
            if bit not in order:
                keep = keep + self.swap(keep, bit)
        return keep

    def gather(self, block, order):
        for bit in reversed(order):
            block = jnp.concatenate([block, self.swap(block, bit)], 0)
        return block


def restore(me, blocks, unpack=None):
    n, high, wide = blocks.shape

    def kernel(scal, source, *targets):
        del scal
        if unpack is None:
            targets[0][...] = source[...]
        else:
            unpack(source, targets)

    if unpack is None:
        shapes = [(high, wide)]
    else:
        shapes = unpack.shapes
    return pl.pallas_call(
        kernel,
        name="restore",
        grid_spec=pltpu.PrefetchScalarGridSpec(
            num_scalar_prefetch=1,
            grid=(n,),
            in_specs=[pl.BlockSpec((None, high, wide), lambda p, me: (p, 0, 0))],
            out_specs=[pl.BlockSpec(s, lambda p, me: (p ^ me[0], 0)) for s in shapes],
        ),
        out_shape=[jax.ShapeDtypeStruct((n * s[0], s[1]), F32) for s in shapes],
    )(me.reshape(1), blocks)


class Unpack:
    def __init__(self, high_q, high_o, width, model):
        self.high_q, self.high_o, self.width = high_q, high_o, width
        self.shapes = [(high_q, width), (high_o, model)]

    def __call__(self, source, targets):
        targets[0][...] = source[0 : self.high_q, :]
        for c in range(self.shapes[1][1] // self.width):
            start = self.high_q + c * self.high_o
            targets[1][:, c * self.width : (c + 1) * self.width] = source[
                start : start + self.high_o, :
            ]


def shards(
    dp_size,
    block_input,
    image_counts,
    first_norm_gain,
    first_norm_bias,
    w_qkv,
    qv_bias,
    w_out,
    b_out,
    second_norm_gain,
    second_norm_bias,
    w_fc1,
    b_fc1,
    w_fc2,
    b_fc2,
    cotangent,
):
    images, seq, model = block_input.shape
    width = w_qkv.shape[2]
    hidden = w_fc1.shape[1]
    rows = -(-seq // 16) * 16
    steps = images // IB
    tokens = images * rows
    net = Exchange(dp_size)
    index = lax.axis_index("dp").astype(jnp.int32)
    order_a = order_b = order_c = (0, 1, 2, 3)
    near = (0,)
    pieces = 1 << len(near)
    blocks = 1 << len(order_a)
    half = blocks // 2
    me_near = net.relative(index, near[::-1])
    me_a, me_b, me_c = (net.relative(index, o) for o in (order_a, order_b, order_c))
    scal = jnp.stack(
        [image_counts[0].astype(jnp.int32), me_near, me_a, me_b, me_near, me_c]
    )
    row = lambda v: v.reshape(1, -1)

    def cross(value):
        return lax.ppermute(value, "tensor", [(0, 1), (1, 0)])

    def fetch(weights):
        shapes = []
        for w in weights:
            shape = list(w.shape)
            shape[-2] //= pieces
            shapes.append(tuple(shape))
        mine = pl.pallas_call(
            functools.partial(portion_kernel, len(weights)),
            name="portion",
            in_specs=[pl.BlockSpec(memory_space=pltpu.SMEM)]
            + [pl.BlockSpec(memory_space=pltpu.VMEM)] * len(weights),
            out_specs=[pl.BlockSpec(memory_space=pltpu.VMEM)] * len(weights),
            out_shape=[jax.ShapeDtypeStruct(s, F32) for s in shapes],
        )(me_near.reshape(1), *weights)
        held = [[cross(m)] for m in mine]
        for bit in near:
            held = [h + [net.swap(piece, bit) for piece in h] for h in held]
        return held

    wq_o, wo_o = fetch([w_qkv, w_out])
    fc1_o, fc2_o = fetch([w_fc1, w_fc2])
    qv_o, bfc1_o = cross(qv_bias), cross(b_fc1)

    flop = 2.0 * tokens * model
    n1, qkv, ctx, part, g = _call(
        first_kernel,
        "first",
        steps,
        scal,
        [
            (block_input, _images(seq, model)),
            (cotangent, _images(seq, model)),
            (row(first_norm_gain), _whole((1, model))),
            (row(first_norm_bias), _whole((1, model))),
            (w_qkv, _whole(w_qkv.shape)),
            (qv_bias, _whole(qv_bias.shape)),
            (w_out, _whole(w_out.shape)),
        ],
        [
            ((images, rows, model), BF16, _images(rows, model)),
            ((images, rows, 3 * width), BF16, _images(rows, 3 * width)),
            ((images, rows, width), BF16, _images(rows, width)),
            ((images, rows, model), F32, _images(rows, model)),
            ((images, rows, model), BF16, _images(rows, model)),
        ],
        [pltpu.VMEM((IB * rows, model), BF16), pltpu.VMEM((model, 3 * width), BF16)],
        flop * 5 * width,
    )
    qkv2, ctx2, wcat2, wout2, resid, n2 = _call(
        functools.partial(second_kernel, pieces),
        "second",
        steps,
        scal,
        [
            (n1, _images(rows, model)),
            (block_input, _images(seq, model)),
            (part, _images(rows, model)),
            (qv_o, _whole(qv_o.shape)),
            (row(b_out), _whole((1, model))),
            (row(second_norm_gain), _whole((1, model))),
            (row(second_norm_bias), _whole((1, model))),
        ]
        + [(w, _whole(w.shape)) for w in wq_o]
        + [(w, _whole(w.shape)) for w in wo_o],
        [
            ((images, rows, 3 * width), BF16, _images(rows, 3 * width)),
            ((images, rows, width), BF16, _images(rows, width)),
            ((model, 3 * width), BF16, _acc((model, 3 * width))),
            ((width, model), BF16, _acc((width, model))),
            ((images, rows, model), F32, _images(rows, model)),
            ((images, rows, model), BF16, _images(rows, model)),
        ],
        [pltpu.VMEM((IB * rows, model), BF16)],
        flop * 5 * width,
    )
    del ctx2
    act, slope, send_a, keep_a = _call(
        mlp_a_kernel,
        "mlp_a",
        steps,
        scal,
        [
            (n2, _images(rows, model)),
            (w_fc1, _whole(w_fc1.shape)),
            (row(b_fc1), _whole((1, hidden))),
            (g.reshape(tokens, model), _whole((tokens, model))),
        ],
        [
            ((images, rows, hidden), BF16, _images(rows, hidden)),
            ((images, rows, hidden), F32, _images(rows, hidden)),
            ((half, hidden // blocks, model), F32, _acc((half, hidden // blocks, model))),
            ((half, hidden // blocks, model), F32, _acc((half, hidden // blocks, model))),
        ],
        [pltpu.VMEM((tokens, hidden), BF16), pltpu.VMEM((hidden, model), F32)],
        flop * 2 * hidden,
    )
    mlp_p, gn2_p, send_b, keep_b, gb1 = _call(
        mlp_b_kernel,
        "mlp_b",
        steps,
        scal,
        [
            (act, _images(rows, hidden)),
            (slope, _images(rows, hidden)),
            (g, _images(rows, model)),
            (n2.reshape(tokens, model), _whole((tokens, model))),
            (w_fc1, _whole(w_fc1.shape)),
            (w_fc2, _whole(w_fc2.shape)),
        ],
        [
            ((images, rows, model), F32, _images(rows, model)),
            ((images, rows, model), F32, _images(rows, model)),
            ((half, model // blocks, hidden), F32, _acc((half, model // blocks, hidden))),
            ((half, model // blocks, hidden), F32, _acc((half, model // blocks, hidden))),
            ((1, hidden), F32, _acc((1, hidden))),
        ],
        [pltpu.VMEM((tokens, hidden), BF16), pltpu.VMEM((model, hidden), F32)],
        flop * 4 * hidden,
    )
    block_out, gr, grb, sums2 = _call(
        functools.partial(mlp_c_kernel, pieces),
        "mlp_c",
        steps,
        scal,
        [
            (n2, _images(rows, model)),
            (g, _images(rows, model)),
            (resid, _images(rows, model)),
            (mlp_p, _images(rows, model)),
            (gn2_p, _images(rows, model)),
            (row(bfc1_o), _whole((1, hidden))),
            (row(second_norm_gain), _whole((1, model))),
            (row(b_fc2), _whole((1, model))),
        ]
        + [(w, _whole(w.shape)) for w in fc1_o]
        + [(w, _whole(w.shape)) for w in fc2_o],
        [
            ((images, seq, model), BF16, _images(seq, model)),
            ((images, rows, model), F32, _images(rows, model)),
            ((images, rows, model), BF16, _images(rows, model)),
            ((8, model), F32, _acc((8, model))),
        ],
        [
            pltpu.VMEM((model, hidden), BF16),
            pltpu.VMEM((hidden, model), BF16),
            pltpu.VMEM((IB * rows, hidden), BF16),
            pltpu.VMEM((IB * rows, hidden), BF16),
        ],
        flop * 4 * hidden,
    )
    packed = (3 * model + model) // blocks
    gn1_p, send_c, keep_c, gqv = _call(
        functools.partial(own_backward_kernel, seq),
        "own_backward",
        steps,
        scal,
        [
            (grb, _images(rows, model)),
            (qkv, _images(rows, 3 * width)),
            (w_qkv, _whole(w_qkv.shape)),
            (w_out, _whole(w_out.shape)),
            (n1.reshape(tokens, model), _whole((tokens, model))),
            (ctx.reshape(tokens, width), _whole((tokens, width))),
            (grb.reshape(tokens, model), _whole((tokens, model))),
        ],
        [
            ((images, rows, model), F32, _images(rows, model)),
            ((half, packed, width), F32, _acc((half, packed, width))),
            ((half, packed, width), F32, _acc((half, packed, width))),
            ((2, width), F32, _acc((2, width))),
        ],
        [
            pltpu.VMEM((tokens, 3 * width), BF16),
            pltpu.VMEM((model, 3 * width), BF16),
            pltpu.VMEM((3 * model, width), F32),
            pltpu.VMEM((width, model), F32),
        ],
        flop * 10 * width,
    )
    gin, sums1 = _call(
        other_backward_kernel,
        "other_backward",
        steps,
        scal,
        [
            (grb, _images(rows, model)),
            (qkv2, _images(rows, 3 * width)),
            (wcat2, _whole(wcat2.shape)),
            (wout2, _whole(wout2.shape)),
            (gn1_p, _images(rows, model)),
            (gr, _images(rows, model)),
            (block_input, _images(seq, model)),
            (row(first_norm_gain), _whole((1, model))),
        ],
        [
            ((images, seq, model), BF16, _images(seq, model)),
            ((8, model), F32, _acc((8, model))),
        ],
        [
            pltpu.VMEM((IB * rows, 3 * width), BF16),
            pltpu.VMEM((IB * rows, model), BF16),
        ],
        flop * 6 * width,
    )

    def total(send, keep, order):
        return net.gather(net.reduce(send, keep, order), order)

    (grad_fc2,) = restore(me_a, total(send_a, keep_a, order_a))
    (grad_fc1,) = restore(me_b, total(send_b, keep_b, order_b))
    grad_qkv, grad_out = restore(
        me_c,
        total(send_c, keep_c, order_c),
        Unpack(3 * model // blocks, width // blocks, width, model),
    )
    small = jnp.concatenate(
        [sums1[0:2].ravel(), sums2[0:4].ravel(), gqv.ravel(), gb1.ravel()]
    )
    pad = -small.size % (8 * LANES)
    small = jnp.pad(small, (0, pad)).reshape(-1, LANES)
    for bit in range(net.bits):
        small = small + net.swap(small, bit)
    small = small.ravel()
    cut = lambda start, size: small[start : start + size]
    base = 6 * model
    return (
        block_out,
        gin,
        cut(0, model),
        cut(model, model),
        grad_qkv.reshape(3, model, width),
        cut(base, 2 * width).reshape(2, width),
        grad_out,
        cut(4 * model, model),
        cut(2 * model, model),
        cut(3 * model, model),
        grad_fc1,
        cut(base + 2 * width, hidden),
        grad_fc2,
        cut(5 * model, model),
    )


def solution(mesh):
    in_specs = (
        P("dp", None, None),
        P("dp"),
        P(),
        P(),
        P(None, None, "tensor"),
        P(None, "tensor"),
        P("tensor", None),
        P(),
        P(),
        P(),
        P(None, "tensor"),
        P("tensor"),
        P("tensor", None),
        P(),
        P("dp", None, None),
    )
    out_specs = (
        P("dp", None, None),
        P("dp", None, None),
        P(),
        P(),
        P(None, None, "tensor"),
        P(None, "tensor"),
        P("tensor", None),
        P(),
        P(),
        P(),
        P(None, "tensor"),
        P("tensor"),
        P("tensor", None),
        P(),
    )
    return jax.shard_map(
        functools.partial(shards, mesh.shape["dp"]),
        mesh=mesh,
        in_specs=in_specs,
        out_specs=out_specs,
        check_vma=False,
    )
```

time: 1200 us -> 654 us (0.55)
  waiting for transfers between devices: 789 us -> 299 us
  Pallas kernels: 0 us -> 249 us
  matrix products: 128 us -> 0 us
  local copies, waits for them, and re-layouts: 135 us -> 32.9 us
  blocking collectives: 61.7 us -> 0 us
  starting transfers between devices: 0.16 us -> 38.8 us
  other arithmetic: 60.7 us -> 24.5 us
  between operations: 15.4 us -> 1.76 us
    psum x4 -> x0, waiting for transfers between devices: 789 us -> none  [the longest x1 276 us: shards(): mlp_full = lax.psum(mlp_part, 'tensor')]
    ppermute x0 -> x38, waiting for transfers between devices: none -> 299 us  [the longest x32 156 us: swap(): return lax.ppermute(value, 'dp', pairs)]
    pallas_call x0 -> x12, Pallas kernels: none -> 249 us  [the longest x7 211 us: _call(): pl.pallas_call(kernel, name=name, grid_spec=pltpu.PrefetchScalarGridSpec(...]
    dot_general x18 -> x0, matrix products: 128 us -> none  [the longest x1 12.1 us: shards(): jnp.einsum('ishd,ithd->ihst', grad_context, values_all, preferred_element...]
    psum x1 -> x0, blocking collectives: 61.7 us -> none  [shards(): lax.psum((first_norm_gain_gradient, grad_ln1_bias, grad_w_qkv, grad_qv_bi...]
    ppermute x0 -> x38, starting transfers between devices: none -> 38.8 us  [the longest x32 28.8 us: swap(): return lax.ppermute(value, 'dp', pairs)]
    reduce_sum x9 -> x0, other arithmetic: 34.2 us -> none  [the longest x2 7.6 us: apply_layer_norm(): center = jnp.mean(values, -1, keepdims=True)]
    another operation x9 -> x1, local copies, waits for them, and re-layouts: 34.6 us -> 0.6 us  [shards(): jnp.stack([image_counts[0].astype(jnp.int32), me_near, me_a, me_b, me_nea...]
  transfers between devices with their start and end apart: 4 -> 38, of which waited for: 4 -> 15; matrix products, arithmetic and copies ran while one was open for 4% -> 8% of each run, Pallas kernels for 0% -> 36%
where the time goes in v1:
time: 654 us; the launch traced here: 647 us
  waiting for transfers between devices  299 us (46%)
  Pallas kernels  249 us (38%)
  starting transfers between devices  38.8 us (6%)
  local copies, waits for them, and re-layouts  32.9 us (5%)
  other arithmetic  24.5 us (4%)
    pallas_call x7, Pallas kernels, _call(): pl.pallas_call(kernel, name=name, grid_spec=pltpu.PrefetchScalarGridSpec(...  211 us
    ppermute x32, waiting for transfers between devices, swap(): return lax.ppermute(value, 'dp', pairs)  156 us
    ppermute x6, waiting for transfers between devices, cross(): return lax.ppermute(value, 'tensor', [(0, 1), (1, 0)])  144 us
    pallas_call x3, Pallas kernels, restore(): pl.pallas_call(kernel, name='restore', grid_spec=pltpu.PrefetchScalarGrid...  30.9 us
    ppermute x32, starting transfers between devices, swap(): return lax.ppermute(value, 'dp', pairs)  28.8 us
    concatenate x9, other arithmetic, gather(): block = jnp.concatenate([block, self.swap(block, bit)], 0)  14.4 us
  transfers between devices with their start and end apart: 38, of which 15 were waited for; matrix products, arithmetic and copies ran while one was open for 8% of the time, Pallas kernels for 36%

profile of v1, /device:TPU:0, one launch (start us, length us, event | category | flops | bytes accessed | tf_op | source)
XLA Modules:
  0.0 646.8 jit_solution(16760297034598690342)
XLA Ops:
  0.7 3.1 portion.2
  3.8 3.0 collective-permute-start.1
  6.8 4.7 portion.3
  13.5 33.0 %collective-permute-done.1.refs_0_ = f32[3,384,384]{2,1,0:T(8,128)} collective-permute-done((f32[3,384,384]{2,1,0:T(8,128)}, f32[3,384,384]{2,1,0:T(8,128)}, u32[]{:S(2)}, u32[]{:S(2)}) %collective-permute-start.1) | collective-permute-done | bytes 1769504 | tf_op jit(solution)/shard_map/ppermute | solution.py:527
  48.6 110.8 %collective-permute-done.3.refs_2_ = f32[192,768]{1,0:T(8,128)S(1)} collective-permute-done((f32[192,768]{1,0:T(8,128)}, f32[192,768]{1,0:T(8,128)S(1)}, u32[]{:S(2)}, u32[]{:S(2)}) %collective-permute-start.3) | collective-permute-done | bytes 589856 | tf_op jit(solution)/shard_map/ppermute | solution.py:527
  164.9 19.8 %first.1 = (bf16[10,208,768]{2,1,0:T(8,128)(2,1)}, bf16[10,208,1152]{2,1,0:T(8,128)(2,1)}, bf16[10,208,384]{2,1,0:T(8,128)(2,1)}, f32[10,208,768]{2,1,0:T(8,128)}, bf16[10,208,768]{2,1,0:T(8,128)(2,1)}) custom-call(s32[6]{0:T(128)} %stack.14.scal, bf16[10,197,768]{2,1,0:T(8,128)(2,1)} %x.7, bf16[10,197,768]{2,1,0:T(8,128)(2,1)} %cot.1, ...), custom_call_target="tpu_custom_call" | custom-call | flops 6134169600 | bytes 16840704 | tf_op jit(solution)/shard_map/first/pallas_call | solution.py:393
  189.6 22.7 %second.1 = (bf16[10,208,1152]{2,1,0:T(8,128)(2,1)}, bf16[10,208,384]{2,1,0:T(8,128)(2,1)}, bf16[768,1152]{1,0:T(8,128)(2,1)}, bf16[384,768]{1,0:T(8,128)(2,1)},...) custom-call(s32[6]{0:T(128)} %stack.14.scal, bf16[10,208,768]{2,1,0:T(8,128)(2,1)} %get-tuple-element.49.n1, ...), custom_call_target="tpu_custom_call" | custom-call | flops 6134169600 | bytes 34682880 | tf_op jit(solution)/shard_map/second/pallas_call | solution.py:393
  212.3 22.8 %mlp_a.1 = (bf16[10,208,1536]{2,1,0:T(8,128)(2,1)}, f32[10,208,1536]{2,1,0:T(8,128)}, f32[8,96,768]{2,1,0:T(8,128)}, f32[8,96,768]{2,1,0:T(8,128)}) custom-call(s32[6]{0:T(128)} %stack.14.scal, bf16[10,208,768]{2,1,0:T(8,128)(2,1)} %get-tuple-element.53.n2, bf16[768,1536]{1,0:T(8,128)(2,1)} %refs_0_.3, f32[1,1536]{1,0:T(1,128)} %reshape.110.bfc1, ...), custom_call_target="tpu_custom_call" | custom-call | flops 9814671360 | bytes 17510400 | tf_op jit(solution)/shard_map/mlp_a/pallas_call | solution.py:393
  235.2 31.0 %mlp_b.1 = (f32[10,208,768]{2,1,0:T(8,128)}, f32[10,208,768]{2,1,0:T(8,128)}, f32[8,48,1536]{2,1,0:T(8,128)}, f32[8,48,1536]{2,1,0:T(8,128)}, f32[1,1536]{1,0:T(1,128)}) custom-call(s32[6]{0:T(128)} %stack.14.scal, bf16[10,208,1536]{2,1,0:T(8,128)(2,1)} %get-tuple-element.56.act, f32[10,208,1536]{2,1,0:T(8,128)} %get-tuple-element.57.slope, ...), custom_call_target="tpu_custom_call" | custom-call | flops 19629342720 | bytes 60555264 | tf_op jit(solution)/shard_map/mlp_b/pallas_call | solution.py:393
  266.8 32.6 %mlp_c.1 = (bf16[10,197,768]{2,1,0:T(8,128)(2,1)}, f32[10,208,768]{2,1,0:T(8,128)}, bf16[10,208,768]{2,1,0:T(8,128)(2,1)}, f32[8,768]{1,0:T(8,128)}) custom-call(s32[6]{0:T(128)} %stack.14.scal, bf16[10,208,768]{2,1,0:T(8,128)(2,1)} %get-tuple-element.53.n2, bf16[10,208,768]{2,1,0:T(8,128)(2,1)} %get-tuple-element.54.g, ...), custom_call_target="tpu_custom_call" | custom-call | flops 19629342720 | bytes 70017024 | tf_op jit(solution)/shard_map/mlp_c/pallas_call | solution.py:393
  299.4 45.4 %own_backward.1 = (f32[10,208,768]{2,1,0:T(8,128)}, f32[8,192,384]{2,1,0:T(8,128)}, f32[8,192,384]{2,1,0:T(8,128)}, f32[2,384]{1,0:T(2,128)}) custom-call(s32[6]{0:T(128)} %stack.14.scal, bf16[10,208,768]{2,1,0:T(8,128)(2,1)} %get-tuple-element.63.grb, bf16[10,208,1152]{2,1,0:T(8,128)(2,1)} %get-tuple-element.67.qkv, bf16[3,768,384]{2,1,0:T(8,128)(2,1)} %w_qkv.3, ...), custom_call_target="tpu_custom_call" | custom-call | flops 12268339200 | bytes 36667392 | tf_op jit(solution)/shard_map/own_backward/pallas_call | solution.py:393
  353.2 22.8 %collective-permute-done.31 = f32[4,96,768]{2,1,0:T(8,128)S(1)} collective-permute-done((f32[4,96,768]{2,1,0:T(8,128)S(1)}, f32[4,96,768]{2,1,0:T(8,128)S(1)}, u32[]{:S(2)}, u32[]{:S(2)}) %collective-permute-start.31) | collective-permute-done | bytes 1179680 | tf_op jit(solution)/shard_map/ppermute | solution.py:420
  377.7 23.5 %collective-permute-done.23 = f32[4,48,1536]{2,1,0:T(8,128)S(1)} collective-permute-done((f32[4,48,1536]{2,1,0:T(8,128)S(1)}, f32[4,48,1536]{2,1,0:T(8,128)S(1)}, u32[]{:S(2)}, u32[]{:S(2)}) %collective-permute-start.23) | collective-permute-done | bytes 1179680 | tf_op jit(solution)/shard_map/ppermute | solution.py:420
  405.7 20.3 %collective-permute-done.15 = f32[4,192,384]{2,1,0:T(8,128)S(1)} collective-permute-done((f32[4,192,384]{2,1,0:T(8,128)S(1)}, f32[4,192,384]{2,1,0:T(8,128)S(1)}, u32[]{:S(2)}, u32[]{:S(2)}) %collective-permute-start.15) | collective-permute-done | bytes 1179680 | tf_op jit(solution)/shard_map/ppermute | solution.py:420
  431.6 21.9 %collective-permute-done.16 = f32[2,192,384]{2,1,0:T(8,128)S(1)} collective-permute-done((f32[2,192,384]{2,1,0:T(8,128)S(1)}, f32[2,192,384]{2,1,0:T(8,128)S(1)}, u32[]{:S(2)}, u32[]{:S(2)}) %collective-permute-start.16) | collective-permute-done | bytes 589856 | tf_op jit(solution)/shard_map/ppermute | solution.py:420
  457.3 10.3 %collective-permute-done.34 = f32[1,96,768]{2,1,0:T(8,128)S(1)} collective-permute-done((f32[1,96,768]{2,1,0:T(8,128)S(1)}, f32[1,96,768]{2,1,0:T(8,128)S(1)}, u32[]{:S(2)}, u32[]{:S(2)}) %collective-permute-start.34) | collective-permute-done | bytes 294944 | tf_op jit(solution)/shard_map/ppermute | solution.py:420
  470.0 5.4 collective-permute-done.17
  476.1 11.7 %collective-permute-done.26 = f32[1,48,1536]{2,1,0:T(8,128)S(1)} collective-permute-done((f32[1,48,1536]{2,1,0:T(8,128)S(1)}, f32[1,48,1536]{2,1,0:T(8,128)S(1)}, u32[]{:S(2)}, u32[]{:S(2)}) %collective-permute-start.26) | collective-permute-done | bytes 294944 | tf_op jit(solution)/shard_map/ppermute | solution.py:420
  489.4 4.7 collective-permute-done.18
  498.2 8.5 %collective-permute-done.27 = f32[2,48,1536]{2,1,0:T(8,128)S(1)} collective-permute-done((f32[2,48,1536]{2,1,0:T(8,128)}, f32[2,48,1536]{2,1,0:T(8,128)S(1)}, u32[]{:S(2)}, u32[]{:S(2)}) %collective-permute-start.27) | collective-permute-done | bytes 589856 | tf_op jit(solution)/shard_map/ppermute | solution.py:420
  509.4 9.9 %collective-permute-done.19 = f32[2,192,384]{2,1,0:T(8,128)S(1)} collective-permute-done((f32[2,192,384]{2,1,0:T(8,128)}, f32[2,192,384]{2,1,0:T(8,128)S(1)}, u32[]{:S(2)}, u32[]{:S(2)}) %collective-permute-start.19) | collective-permute-done | bytes 589856 | tf_op jit(solution)/shard_map/ppermute | solution.py:420
  521.9 36.3 %other_backward.1 = (bf16[10,197,768]{2,1,0:T(8,128)(2,1)}, f32[8,768]{1,0:T(8,128)}) custom-call(s32[6]{0:T(128)} %stack.14.scal, bf16[10,208,768]{2,1,0:T(8,128)(2,1)} %get-tuple-element.63.grb, bf16[10,208,1152]{2,1,0:T(8,128)(2,1)} %get-tuple-element.64.qkv, bf16[768,1152]{1,0:T(8,128)(2,1)} %get-tuple-element.65.wcat, ...), custom_call_target="tpu_custom_call" | custom-call | flops 7361003520 | bytes 52310016 | tf_op jit(solution)/shard_map/other_backward/pallas_call | solution.py:393
  564.8 11.0 %collective-permute-done.11 = f32[56,128]{1,0:T(8,128)S(1)} collective-permute-done((f32[56,128]{1,0:T(8,128)S(1)}, f32[56,128]{1,0:T(8,128)S(1)}, u32[]{:S(2)}, u32[]{:S(2)}) %collective-permute-start.11) | collective-permute-done | bytes 28704 | tf_op jit(solution)/shard_map/ppermute | solution.py:420
  581.2 2.8 pad_maximum_fusion.1
  585.0 4.4 collective-permute-done.13
  589.4 2.8 pad_maximum_fusion
  605.9 3.2 constant_dynamic-update-slice_fusion.10.source
  609.1 10.3 %restore.5 = f32[1536,768]{1,0:T(8,128)} custom-call(s32[1]{0:T(128)} %bitcast.1.scal, f32[16,96,768]{2,1,0:T(8,128)} %constant_dynamic-update-slice_fusion.10.source), custom_call_target="tpu_custom_call" | custom-call | tf_op jit(solution)/shard_map/restore/pallas_call | solution.py:461
  619.4 3.3 constant_dynamic-update-slice_fusion.5.source
  622.7 10.3 %restore.4 = f32[768,1536]{1,0:T(8,128)} custom-call(s32[1]{0:T(128)} %bitcast.1.scal, f32[16,48,1536]{2,1,0:T(8,128)} %constant_dynamic-update-slice_fusion.5.source), custom_call_target="tpu_custom_call" | custom-call | tf_op jit(solution)/shard_map/restore/pallas_call | solution.py:461
  633.0 3.3 constant_dynamic-update-slice_fusion.source
  636.3 10.3 %restore.3 = (f32[2304,384]{1,0:T(8,128)}, f32[384,768]{1,0:T(8,128)}) custom-call(s32[1]{0:T(128)} %bitcast.1.scal, f32[16,192,384]{2,1,0:T(8,128)} %constant_dynamic-update-slice_fusion.source), custom_call_target="tpu_custom_call" | custom-call | tf_op jit(solution)/shard_map/restore/pallas_call | solution.py:461
  (144 shorter events, 79.0 us)
Async XLA Ops:
  3.8 42.8 %collective-permute-start.1 = (f32[3,384,384]{2,1,0:T(8,128)}, f32[3,384,384]{2,1,0:T(8,128)}, u32[]{:S(2)}, u32[]{:S(2)}) collective-permute-start(f32[3,384,384]{2,1,0:T(8,128)} %get-tuple-element.51), channel_id=1, source_target_pairs={{0,1},{1,0},{2,3},{3,2},{4,5},{5,4},{6,7},{7,6},{8,9},{9,8},{10,11... | collective-permute-start | bytes 5308424 | tf_op jit(solution)/shard_map/ppermute | solution.py:527
  11.5 176.7 %collective-permute-start.6 = (f32[384,1536]{1,0:T(8,128)}, f32[384,1536]{1,0:T(8,128)S(1)}, u32[]{:S(2)}, u32[]{:S(2)}) collective-permute-start(f32[384,1536]{1,0:T(8,128)} %get-tuple-element.60), channel_id=1, source_target_pairs={{0,1},{1,0},{2,3},{3,2},{4,5},{5,4},{6,7},{7,6},{8,9},{9,8},{10,11... | collective-permute-start | bytes 7077896 | tf_op jit(solution)/shard_map/ppermute | solution.py:527
  11.5 176.7 %collective-permute-start.8 = (f32[768,768]{1,0:T(8,128)}, f32[768,768]{1,0:T(8,128)}, u32[]{:S(2)}, u32[]{:S(2)}) collective-permute-start(f32[768,768]{1,0:T(8,128)} %get-tuple-element.61), channel_id=1, source_target_pairs={{0,1},{1,0},{2,3},{3,2},{4,5},{5,4},{6,7},{7,6},{8,9},{9,8},{10,11... | collective-permute-start | bytes 7077896 | tf_op jit(solution)/shard_map/ppermute | solution.py:527
  46.6 142.2 %collective-permute-start.2 = (f32[3,384,384]{2,1,0:T(8,128)}, f32[3,384,384]{2,1,0:T(8,128)}, u32[]{:S(2)}, u32[]{:S(2)}) collective-permute-start(f32[3,384,384]{2,1,0:T(8,128)} %collective-permute-done.1.refs_0_), channel_id=1, source_target_pairs={{0,2},{2,0},{4,6},{6,4},{8,10},{10,8},{12,14},{14,12},{16,18},{18,... | collective-permute-start | bytes 5308424 | tf_op jit(solution)/shard_map/ppermute | solution.py:420
  46.6 112.8 %collective-permute-start.3 = (f32[192,768]{1,0:T(8,128)}, f32[192,768]{1,0:T(8,128)S(1)}, u32[]{:S(2)}, u32[]{:S(2)}) collective-permute-start(f32[192,768]{1,0:T(8,128)} %get-tuple-element.52), channel_id=1, source_target_pairs={{0,1},{1,0},{2,3},{3,2},{4,5},{5,4},{6,7},{7,6},{8,9},{9,8},{10,11... | collective-permute-start | bytes 1769480 | tf_op jit(solution)/shard_map/ppermute | solution.py:527
  159.4 29.4 %collective-permute-start.4 = (f32[192,768]{1,0:T(8,128)S(1)}, f32[192,768]{1,0:T(8,128)}, u32[]{:S(2)}, u32[]{:S(2)}) collective-permute-start(f32[192,768]{1,0:T(8,128)S(1)} %collective-permute-done.3.refs_2_), channel_id=1, source_target_pairs={{0,2},{2,0},{4,6},{6,4},{8,10},{10,8},{12,14},{14,12},{16,18},{18,... | collective-permute-start | bytes 1769480 | tf_op jit(solution)/shard_map/ppermute | solution.py:420
  163.7 25.1 %collective-permute-start = (f32[2,384]{1,0:T(2,128)S(1)}, f32[2,384]{1,0:T(2,128)S(1)}, u32[]{:S(2)}, u32[]{:S(2)}) collective-permute-start(f32[2,384]{1,0:T(2,128)S(1)} %copy-done.14), channel_id=1, source_target_pairs={{0,1},{1,0},{2,3},{3,2},{4,5},{5,4},{6,7},{7,6},{8,9},{9,8},{10,11... | collective-permute-start | bytes 9224 | tf_op jit(solution)/shard_map/ppermute | solution.py:527
  188.2 78.5 %collective-permute-start.7 = (f32[384,1536]{1,0:T(8,128)S(1)}, f32[384,1536]{1,0:T(8,128)}, u32[]{:S(2)}, u32[]{:S(2)}) collective-permute-start(f32[384,1536]{1,0:T(8,128)S(1)} %collective-permute-done.6.refs_0_), channel_id=1, source_target_pairs={{0,2},{2,0},{4,6},{6,4},{8,10},{10,8},{12,14},{14,12},{16,18},{18,... | collective-permute-start | bytes 7077896 | tf_op jit(solution)/shard_map/ppermute | solution.py:420
  188.2 78.5 %collective-permute-start.9 = (f32[768,768]{1,0:T(8,128)}, f32[768,768]{1,0:T(8,128)}, u32[]{:S(2)}, u32[]{:S(2)}) collective-permute-start(f32[768,768]{1,0:T(8,128)} %collective-permute-done.8.refs_2_), channel_id=1, source_target_pairs={{0,2},{2,0},{4,6},{6,4},{8,10},{10,8},{12,14},{14,12},{16,18},{18,... | collective-permute-start | bytes 7077896 | tf_op jit(solution)/shard_map/ppermute | solution.py:420
  235.1 109.8 %collective-permute-start.30 = (f32[8,96,768]{2,1,0:T(8,128)}, f32[8,96,768]{2,1,0:T(8,128)}, u32[]{:S(2)}, u32[]{:S(2)}) collective-permute-start(f32[8,96,768]{2,1,0:T(8,128)} %get-tuple-element.83), channel_id=1, source_target_pairs={{0,2},{2,0},{4,6},{6,4},{8,10},{10,8},{12,14},{14,12},{16,18},{18,... | collective-permute-start | bytes 7077896 | tf_op jit(solution)/shard_map/ppermute | solution.py:420
  266.2 82.4 %collective-permute-start.22 = (f32[8,48,1536]{2,1,0:T(8,128)}, f32[8,48,1536]{2,1,0:T(8,128)}, u32[]{:S(2)}, u32[]{:S(2)}) collective-permute-start(f32[8,48,1536]{2,1,0:T(8,128)} %get-tuple-element.81), channel_id=1, source_target_pairs={{0,2},{2,0},{4,6},{6,4},{8,10},{10,8},{12,14},{14,12},{16,18},{18,... | collective-permute-start | bytes 7077896 | tf_op jit(solution)/shard_map/ppermute | solution.py:420
  347.0 28.9 %collective-permute-start.31 = (f32[4,96,768]{2,1,0:T(8,128)S(1)}, f32[4,96,768]{2,1,0:T(8,128)S(1)}, u32[]{:S(2)}, u32[]{:S(2)}) collective-permute-start(f32[4,96,768]{2,1,0:T(8,128)S(1)} %get-tuple-element.91), channel_id=1, source_target_pairs={{0,4},{2,6},{4,0},{6,2},{8,12},{10,14},{12,8},{14,10},{16,20},{18,... | collective-permute-start | bytes 3538952 | tf_op jit(solution)/shard_map/ppermute | solution.py:420
  350.8 50.4 %collective-permute-start.23 = (f32[4,48,1536]{2,1,0:T(8,128)S(1)}, f32[4,48,1536]{2,1,0:T(8,128)S(1)}, u32[]{:S(2)}, u32[]{:S(2)}) collective-permute-start(f32[4,48,1536]{2,1,0:T(8,128)S(1)} %get-tuple-element.93), channel_id=1, source_target_pairs={{0,4},{2,6},{4,0},{6,2},{8,12},{10,14},{12,8},{14,10},{16,20},{18,... | collective-permute-start | bytes 3538952 | tf_op jit(solution)/shard_map/ppermute | solution.py:420
  351.6 74.4 %collective-permute-start.15 = (f32[4,192,384]{2,1,0:T(8,128)S(1)}, f32[4,192,384]{2,1,0:T(8,128)S(1)}, u32[]{:S(2)}, u32[]{:S(2)}) collective-permute-start(f32[4,192,384]{2,1,0:T(8,128)S(1)} %get-tuple-element.95), channel_id=1, source_target_pairs={{0,4},{2,6},{4,0},{6,2},{8,12},{10,14},{12,8},{14,10},{16,20},{18,... | collective-permute-start | bytes 3538952 | tf_op jit(solution)/shard_map/ppermute | solution.py:420
  376.1 26.9 %collective-permute-start.32 = (f32[2,96,768]{2,1,0:T(8,128)S(1)}, f32[2,96,768]{2,1,0:T(8,128)S(1)}, u32[]{:S(2)}, u32[]{:S(2)}) collective-permute-start(f32[2,96,768]{2,1,0:T(8,128)S(1)} %get-tuple-element.97), channel_id=1, source_target_pairs={{0,8},{2,10},{4,12},{6,14},{8,0},{10,2},{12,4},{14,6},{16,24},{18,... | collective-permute-start | bytes 1769480 | tf_op jit(solution)/shard_map/ppermute | solution.py:420
  401.3 26.5 %collective-permute-start.24 = (f32[2,48,1536]{2,1,0:T(8,128)S(1)}, f32[2,48,1536]{2,1,0:T(8,128)S(1)}, u32[]{:S(2)}, u32[]{:S(2)}) collective-permute-start(f32[2,48,1536]{2,1,0:T(8,128)S(1)} %get-tuple-element.99), channel_id=1, source_target_pairs={{0,8},{2,10},{4,12},{6,14},{8,0},{10,2},{12,4},{14,6},{16,24},{18,... | collective-permute-start | bytes 1769480 | tf_op jit(solution)/shard_map/ppermute | solution.py:420
  403.0 27.5 %collective-permute-start.33 = (f32[1,96,768]{2,1,0:T(8,128)S(1)}, f32[1,96,768]{2,1,0:T(8,128)S(1)}, u32[]{:S(2)}, u32[]{:S(2)}) collective-permute-start(f32[1,96,768]{2,1,0:T(8,128)S(1)} %slice_add_fusion.12), channel_id=1, source_target_pairs={{0,16},{2,18},{4,20},{6,22},{8,24},{10,26},{12,28},{14,30},{16,0},... | collective-permute-start | bytes 884744 | tf_op jit(solution)/shard_map/ppermute | solution.py:420
  426.2 27.3 %collective-permute-start.16 = (f32[2,192,384]{2,1,0:T(8,128)S(1)}, f32[2,192,384]{2,1,0:T(8,128)S(1)}, u32[]{:S(2)}, u32[]{:S(2)}) collective-permute-start(f32[2,192,384]{2,1,0:T(8,128)S(1)} %get-tuple-element.101), channel_id=1, source_target_pairs={{0,8},{2,10},{4,12},{6,14},{8,0},{10,2},{12,4},{14,6},{16,24},{18,... | collective-permute-start | bytes 1769480 | tf_op jit(solution)/shard_map/ppermute | solution.py:420
  427.8 26.3 %collective-permute-start.25 = (f32[1,48,1536]{2,1,0:T(8,128)S(1)}, f32[1,48,1536]{2,1,0:T(8,128)S(1)}, u32[]{:S(2)}, u32[]{:S(2)}) collective-permute-start(f32[1,48,1536]{2,1,0:T(8,128)S(1)} %slice_add_fusion.14), channel_id=1, source_target_pairs={{0,16},{2,18},{4,20},{6,22},{8,24},{10,26},{12,28},{14,30},{16,0},... | collective-permute-start | bytes 884744 | tf_op jit(solution)/shard_map/ppermute | solution.py:420
  431.3 36.3 %collective-permute-start.34 = (f32[1,96,768]{2,1,0:T(8,128)S(1)}, f32[1,96,768]{2,1,0:T(8,128)S(1)}, u32[]{:S(2)}, u32[]{:S(2)}) collective-permute-start(f32[1,96,768]{2,1,0:T(8,128)S(1)} %get-tuple-element.85), channel_id=1, source_target_pairs={{0,16},{2,18},{4,20},{6,22},{8,24},{10,26},{12,28},{14,30},{16,0},... | collective-permute-start | bytes 884744 | tf_op jit(solution)/shard_map/ppermute | solution.py:420
  453.5 21.8 %collective-permute-start.17 = (f32[1,192,384]{2,1,0:T(8,128)S(1)}, f32[1,192,384]{2,1,0:T(8,128)S(1)}, u32[]{:S(2)}, u32[]{:S(2)}) collective-permute-start(f32[1,192,384]{2,1,0:T(8,128)S(1)} %slice_add_fusion.16), channel_id=1, source_target_pairs={{0,16},{2,18},{4,20},{6,22},{8,24},{10,26},{12,28},{14,30},{16,0},... | collective-permute-start | bytes 884744 | tf_op jit(solution)/shard_map/ppermute | solution.py:420
  454.9 32.8 %collective-permute-start.26 = (f32[1,48,1536]{2,1,0:T(8,128)S(1)}, f32[1,48,1536]{2,1,0:T(8,128)S(1)}, u32[]{:S(2)}, u32[]{:S(2)}) collective-permute-start(f32[1,48,1536]{2,1,0:T(8,128)S(1)} %get-tuple-element.87), channel_id=1, source_target_pairs={{0,16},{2,18},{4,20},{6,22},{8,24},{10,26},{12,28},{14,30},{16,0},... | collective-permute-start | bytes 884744 | tf_op jit(solution)/shard_map/ppermute | solution.py:420
  468.4 27.2 %collective-permute-start.35 = (f32[2,96,768]{2,1,0:T(8,128)}, f32[2,96,768]{2,1,0:T(8,128)S(1)}, u32[]{:S(2)}, u32[]{:S(2)}) collective-permute-start(f32[2,96,768]{2,1,0:T(8,128)} %pad_maximum_fusion.8), channel_id=1, source_target_pairs={{0,8},{2,10},{4,12},{6,14},{8,0},{10,2},{12,4},{14,6},{16,24},{18,... | collective-permute-start | bytes 1769480 | tf_op jit(solution)/shard_map/ppermute | solution.py:420
  476.1 18.0 %collective-permute-start.18 = (f32[1,192,384]{2,1,0:T(8,128)S(1)}, f32[1,192,384]{2,1,0:T(8,128)S(1)}, u32[]{:S(2)}, u32[]{:S(2)}) collective-permute-start(f32[1,192,384]{2,1,0:T(8,128)S(1)} %get-tuple-element.89), channel_id=1, source_target_pairs={{0,16},{2,18},{4,20},{6,22},{8,24},{10,26},{12,28},{14,30},{16,0},... | collective-permute-start | bytes 884744 | tf_op jit(solution)/shard_map/ppermute | solution.py:420
  488.6 18.1 %collective-permute-start.27 = (f32[2,48,1536]{2,1,0:T(8,128)}, f32[2,48,1536]{2,1,0:T(8,128)S(1)}, u32[]{:S(2)}, u32[]{:S(2)}) collective-permute-start(f32[2,48,1536]{2,1,0:T(8,128)} %pad_maximum_fusion.7), channel_id=1, source_target_pairs={{0,8},{2,10},{4,12},{6,14},{8,0},{10,2},{12,4},{14,6},{16,24},{18,... | collective-permute-start | bytes 1769480 | tf_op jit(solution)/shard_map/ppermute | solution.py:420
  495.0 24.3 %collective-permute-start.19 = (f32[2,192,384]{2,1,0:T(8,128)}, f32[2,192,384]{2,1,0:T(8,128)S(1)}, u32[]{:S(2)}, u32[]{:S(2)}) collective-permute-start(f32[2,192,384]{2,1,0:T(8,128)} %pad_maximum_fusion.6), channel_id=1, source_target_pairs={{0,8},{2,10},{4,12},{6,14},{8,0},{10,2},{12,4},{14,6},{16,24},{18,... | collective-permute-start | bytes 1769480 | tf_op jit(solution)/shard_map/ppermute | solution.py:420
  496.7 81.6 %collective-permute-start.36 = (f32[4,96,768]{2,1,0:T(8,128)}, f32[4,96,768]{2,1,0:T(8,128)}, u32[]{:S(2)}, u32[]{:S(2)}) collective-permute-start(f32[4,96,768]{2,1,0:T(8,128)} %pad_maximum_fusion.5), channel_id=1, source_target_pairs={{0,4},{2,6},{4,0},{6,2},{8,12},{10,14},{12,8},{14,10},{16,20},{18,... | collective-permute-start | bytes 3538952 | tf_op jit(solution)/shard_map/ppermute | solution.py:420
  507.9 73.3 %collective-permute-start.28 = (f32[4,48,1536]{2,1,0:T(8,128)}, f32[4,48,1536]{2,1,0:T(8,128)}, u32[]{:S(2)}, u32[]{:S(2)}) collective-permute-start(f32[4,48,1536]{2,1,0:T(8,128)} %pad_maximum_fusion.4), channel_id=1, source_target_pairs={{0,4},{2,6},{4,0},{6,2},{8,12},{10,14},{12,8},{14,10},{16,20},{18,... | collective-permute-start | bytes 3538952 | tf_op jit(solution)/shard_map/ppermute | solution.py:420
  520.3 69.0 %collective-permute-start.20 = (f32[4,192,384]{2,1,0:T(8,128)}, f32[4,192,384]{2,1,0:T(8,128)}, u32[]{:S(2)}, u32[]{:S(2)}) collective-permute-start(f32[4,192,384]{2,1,0:T(8,128)} %pad_maximum_fusion.3), channel_id=1, source_target_pairs={{0,4},{2,6},{4,0},{6,2},{8,12},{10,14},{12,8},{14,10},{16,20},{18,... | collective-permute-start | bytes 3538952 | tf_op jit(solution)/shard_map/ppermute | solution.py:420
  581.1 24.8 %collective-permute-start.37 = (f32[8,96,768]{2,1,0:T(8,128)}, f32[8,96,768]{2,1,0:T(8,128)}, u32[]{:S(2)}, u32[]{:S(2)}) collective-permute-start(f32[8,96,768]{2,1,0:T(8,128)} %pad_maximum_fusion.2), channel_id=1, source_target_pairs={{0,2},{2,0},{4,6},{6,4},{8,10},{10,8},{12,14},{14,12},{16,18},{18,... | collective-permute-start | bytes 7077896 | tf_op jit(solution)/shard_map/ppermute | solution.py:420
  584.0 35.5 %collective-permute-start.29 = (f32[8,48,1536]{2,1,0:T(8,128)}, f32[8,48,1536]{2,1,0:T(8,128)}, u32[]{:S(2)}, u32[]{:S(2)}) collective-permute-start(f32[8,48,1536]{2,1,0:T(8,128)} %pad_maximum_fusion.1), channel_id=1, source_target_pairs={{0,2},{2,0},{4,6},{6,4},{8,10},{10,8},{12,14},{14,12},{16,18},{18,... | collective-permute-start | bytes 7077896 | tf_op jit(solution)/shard_map/ppermute | solution.py:420
  592.2 40.8 %collective-permute-start.21 = (f32[8,192,384]{2,1,0:T(8,128)}, f32[8,192,384]{2,1,0:T(8,128)}, u32[]{:S(2)}, u32[]{:S(2)}) collective-permute-start(f32[8,192,384]{2,1,0:T(8,128)} %pad_maximum_fusion), channel_id=1, source_target_pairs={{0,2},{2,0},{4,6},{6,4},{8,10},{10,8},{12,14},{14,12},{16,18},{18,... | collective-permute-start | bytes 7077896 | tf_op jit(solution)/shard_map/ppermute | solution.py:420
  (22 other events, 938.7 us)
